TPU v7x, 32 devices: a whole 2x2x4 slice. The times are simulated.
32 devices in a mesh: sec: 4 (over x, core), row: 4 (over z), col: 2 (over y).
Axes of the slice: x: 2, y: 2, z: 4, core: 2. Of those that a mesh axis runs over, the one named last changes fastest.
Arguments:
- forcing: float32 [4, 8192, 128], P('sec', ('row', 'col')), may hold values from -6 to 6
- inverse_factor: bfloat16 [4, 2, 8192, 8192], P('sec', None, 'col', 'row'), as said below
- diag_inverse: float32 [4, 2, 8192], P('sec', None, 'col'), may hold values from -0.6 to 0.6
- coupling: float32 [4, 2, 8192], P('sec', None, ('row', 'col')), may hold values from -0.8 to 0.8
Outputs:
- section_fields: float32 [4, 8192, 128], P('sec', ('row', 'col'))
Inputs may be any that keep to these rules, and one draw needn't show every extreme that they name: `inverse_factor`: each section's factor is lower triangular: entries above the diagonal are zero in both parts.
All inputs are finite; a program needn't handle non-finite values.
Results may differ from a plain program's by a relative error of at most 0.03.
Values may be sent and summed in bfloat16 or wider, within the bound.
A program may use at most 128 MiB of HBM per device.

v0:
```python
import jax
import jax.numpy as jnp
from jax import lax
from jax.sharding import PartitionSpec as P


def shifted(value, axis, steps):
    count = lax.axis_size(axis)
    initial, last = (max(0, -steps), min(count, count - steps))
    return lax.ppermute(value, axis, [(source, source + steps) for source in range(initial, last)])


def complex_rows(coef_re, coef_im, values, half):
    v_re = values[:, :half]
    v_im = values[:, half:]
    out_re = coef_re[:, None] * v_re - coef_im[:, None] * v_im
    out_im = coef_re[:, None] * v_im + coef_im[:, None] * v_re
    return jnp.concatenate([out_re, out_im], axis=1)


def combine_stack(product):
    half = product.shape[2] // 2
    out_re = product[0, :, :half] - product[1, :, half:]
    out_im = product[0, :, half:] + product[1, :, :half]
    return jnp.concatenate([out_re, out_im], axis=1)


def solve_section(source, factor, dinv):
    width = source.shape[1]
    product = jnp.einsum(
        "kij,jb->kib",
        factor,
        lax.all_gather(source, "col", axis=0, tiled=True),
        preferred_element_type=jnp.float32,
    )
    forward = combine_stack(product)
    share = lax.psum_scatter(
        forward.astype(jnp.bfloat16), "row", scatter_dimension=0, tiled=True
    ).astype(jnp.float32)
    share_rows = share.shape[0]
    local_dinv = lax.dynamic_slice_in_dim(dinv, lax.axis_index("row") * share_rows, share_rows, 1)
    scaled = complex_rows(local_dinv[0], local_dinv[1], share, width // 2).astype(jnp.bfloat16)
    product = jnp.einsum(
        "kij,ib->kjb",
        factor,
        lax.all_gather(scaled, "row", axis=0, tiled=True),
        preferred_element_type=jnp.float32,
    )
    back = combine_stack(product)
    return lax.psum_scatter(
        back.astype(jnp.bfloat16), "col", scatter_dimension=0, tiled=True
    ).astype(jnp.float32)


def local(forcing, inverse_factor, diag_inverse, coupling):
    sections = lax.axis_size("sec")
    section_id = lax.axis_index("sec")
    local_rhs = forcing[0]
    factor = inverse_factor[0]
    dinv = diag_inverse[0]
    couple = coupling[0]
    rows_here = local_rhs.shape[0]
    half = local_rhs.shape[1] // 2
    block_count = 1
    block_width = half // block_count
    rhs_blocks = local_rhs.reshape(rows_here, 2, block_count, block_width)
    results = jnp.zeros((rows_here, 2, block_count, block_width), jnp.float32)
    outgoing = jnp.zeros((rows_here, 2 * block_width), jnp.float32)
    for step_index in range(block_count + sections - 1):
        if step_index > 0:
            incoming = shifted(outgoing.astype(jnp.bfloat16), "sec", 1).astype(outgoing.dtype)
        else:
            incoming = jnp.zeros((rows_here, 2 * block_width), jnp.float32)
        block_index = step_index - section_id
        active = jnp.logical_and(block_index >= 0, block_index < block_count)
        safe_index = jnp.clip(block_index, 0, block_count - 1)
        current = lax.dynamic_index_in_dim(rhs_blocks, safe_index, 2, keepdims=False)
        current = current.reshape(rows_here, 2 * block_width)
        source = (current - complex_rows(couple[0], couple[1], incoming, block_width)).astype(
            jnp.bfloat16
        )
        field = solve_section(source, factor, dinv)
        updated = lax.dynamic_update_index_in_dim(
            results, field.reshape(rows_here, 2, block_width), safe_index, 2
        )
        results = jnp.where(active, updated, results)
        outgoing = field
    return results.reshape(1, rows_here, 2 * half)


def solution(mesh):
    placed = (
        P("sec", ("row", "col"), None),
        P("sec", None, "col", "row"),
        P("sec", None, "col"),
        P("sec", None, ("row", "col")),
    )
    return jax.shard_map(
        local, mesh=mesh, in_specs=placed, out_specs=P("sec", ("row", "col"), None), check_vma=False
    )
```

profile of v0, /device:TPU:3, one launch (start us, length us, event | category | flops | bytes accessed | tf_op | source)
XLA Modules:
  0.0 480.7 jit_solution(10238314074252563666)
XLA Ops:
  8.7 7.9 %all_gather.24 = bf16[2048,128]{0,1:T(8,128)(2,1)S(1)} all-gather(bf16[1024,128]{0,1:T(8,128)(2,1)S(1)} %fusion.68), channel_id=1, replica_groups=mesh['sec'=4,'row'=4,'col'=2] {'col'}, dimensions={0}, use_global_device_ids=true | all-gather | bytes 786432 | tf_op jit(solution)/shard_map/all_gather | solution.py:33
  16.6 16.3 %fusion.16 = f32[2,4096,128]{1,2,0:T(8,128)S(1)} fusion(bf16[1,2,4096,2048]{3,2,1,0:T(8,128)(2,1)} %param.5, bf16[2048,128]{0,1:T(8,128)(2,1)S(1)} %all_gather.24), kind=kOutput, calls=%fused_computation.16 | convolution fusion | flops 4294967296 | bytes 38273024 | tf_op jit(solution)/shard_map/kij,jb->kib/dot_general | solution.py:30
  35.1 28.4 %reduce-scatter.9.cloned.1.call-done = bf16[1024,128]{0,1:T(8,128)(2,1)} async-done(((bf16[4096,128]{0,1:T(8,128)(2,1)}), bf16[1024,128]{0,1:T(8,128)(2,1)}) %reduce-scatter.9.cloned.1.call-update) | async-done | bytes 262160 | tf_op jit(solution)/shard_map/reduce_scatter | solution.py:37
  65.3 26.7 %all-gather.5.cloned.1.call-done = bf16[4096,128]{0,1:T(8,128)(2,1)} async-done(((bf16[1024,128]{0,1:T(8,128)(2,1)}), bf16[4096,128]{0,1:T(8,128)(2,1)}) %all-gather.5.cloned.1.call-update) | async-done | bytes 1048592 | tf_op jit(solution)/shard_map/all_gather | solution.py:46
  92.0 13.2 %fusion.28 = f32[2,2048,128]{1,2,0:T(8,128)S(1)} fusion(bf16[1,2,4096,2048]{3,2,1,0:T(8,128)(2,1)} %param.5, bf16[4096,128]{0,1:T(8,128)(2,1)} %all-gather.5.cloned.1.call-done), kind=kOutput, calls=%fused_computation.20 | convolution fusion | flops 4294967296 | bytes 36700160 | tf_op jit(solution)/shard_map/kij,ib->kjb/dot_general | solution.py:43
  106.3 14.3 %reduce-scatter.11.cloned.1.call-done = bf16[1024,128]{0,1:T(8,128)(2,1)} async-done(((bf16[2048,128]{0,1:T(8,128)(2,1)}), bf16[1024,128]{0,1:T(8,128)(2,1)}) %reduce-scatter.11.cloned.1.call-update) | async-done | bytes 262160 | tf_op jit(solution)/shard_map/reduce_scatter | solution.py:50
  124.6 5.9 %all_gather.26 = bf16[2048,128]{0,1:T(8,128)(2,1)S(1)} all-gather(bf16[1024,128]{0,1:T(8,128)(2,1)S(1)} %fusion.69), channel_id=1, replica_groups=mesh['sec'=4,'row'=4,'col'=2] {'col'}, dimensions={0}, use_global_device_ids=true | all-gather | bytes 786432 | tf_op jit(solution)/shard_map/all_gather | solution.py:33
  130.5 16.3 %fusion.19 = f32[2,4096,128]{1,2,0:T(8,128)S(1)} fusion(bf16[1,2,4096,2048]{3,2,1,0:T(8,128)(2,1)} %param.5, bf16[2048,128]{0,1:T(8,128)(2,1)S(1)} %all_gather.26), kind=kOutput, calls=%fused_computation.17 | convolution fusion | flops 4294967296 | bytes 38273024 | tf_op jit(solution)/shard_map/kij,jb->kib/dot_general | solution.py:30
  148.1 32.3 %reduce-scatter.13.cloned.1.call-done = bf16[1024,128]{0,1:T(8,128)(2,1)} async-done(((bf16[4096,128]{0,1:T(8,128)(2,1)}), bf16[1024,128]{0,1:T(8,128)(2,1)}) %reduce-scatter.13.cloned.1.call-update) | async-done | bytes 262160 | tf_op jit(solution)/shard_map/reduce_scatter | solution.py:37
  182.5 26.5 %all-gather.7.cloned.1.call-done = bf16[4096,128]{0,1:T(8,128)(2,1)} async-done(((bf16[1024,128]{0,1:T(8,128)(2,1)}), bf16[4096,128]{0,1:T(8,128)(2,1)}) %all-gather.7.cloned.1.call-update) | async-done | bytes 1048592 | tf_op jit(solution)/shard_map/all_gather | solution.py:46
  209.0 13.2 %fusion.31 = f32[2,2048,128]{1,2,0:T(8,128)S(1)} fusion(bf16[1,2,4096,2048]{3,2,1,0:T(8,128)(2,1)} %param.5, bf16[4096,128]{0,1:T(8,128)(2,1)} %all-gather.7.cloned.1.call-done), kind=kOutput, calls=%fused_computation.21 | convolution fusion | flops 4294967296 | bytes 36700160 | tf_op jit(solution)/shard_map/kij,ib->kjb/dot_general | solution.py:43
  223.2 14.3 %reduce-scatter.15.cloned.1.call-done = bf16[1024,128]{0,1:T(8,128)(2,1)} async-done(((bf16[2048,128]{0,1:T(8,128)(2,1)}), bf16[1024,128]{0,1:T(8,128)(2,1)}) %reduce-scatter.15.cloned.1.call-update) | async-done | bytes 262160 | tf_op jit(solution)/shard_map/reduce_scatter | solution.py:50
  241.5 5.9 %all_gather.28 = bf16[2048,128]{0,1:T(8,128)(2,1)S(1)} all-gather(bf16[1024,128]{0,1:T(8,128)(2,1)S(1)} %fusion.70), channel_id=1, replica_groups=mesh['sec'=4,'row'=4,'col'=2] {'col'}, dimensions={0}, use_global_device_ids=true | all-gather | bytes 786432 | tf_op jit(solution)/shard_map/all_gather | solution.py:33
  247.4 16.3 %fusion.22 = f32[2,4096,128]{1,2,0:T(8,128)S(1)} fusion(bf16[1,2,4096,2048]{3,2,1,0:T(8,128)(2,1)} %param.5, bf16[2048,128]{0,1:T(8,128)(2,1)S(1)} %all_gather.28), kind=kOutput, calls=%fused_computation.18 | convolution fusion | flops 4294967296 | bytes 38273024 | tf_op jit(solution)/shard_map/kij,jb->kib/dot_general | solution.py:30
  265.1 32.3 %reduce-scatter.17.cloned.1.call-done = bf16[1024,128]{0,1:T(8,128)(2,1)} async-done(((bf16[4096,128]{0,1:T(8,128)(2,1)}), bf16[1024,128]{0,1:T(8,128)(2,1)}) %reduce-scatter.17.cloned.1.call-update) | async-done | bytes 262160 | tf_op jit(solution)/shard_map/reduce_scatter | solution.py:37
  299.3 26.7 %all-gather.9.cloned.1.call-done = bf16[4096,128]{0,1:T(8,128)(2,1)} async-done(((bf16[1024,128]{0,1:T(8,128)(2,1)}), bf16[4096,128]{0,1:T(8,128)(2,1)}) %all-gather.9.cloned.1.call-update) | async-done | bytes 1048592 | tf_op jit(solution)/shard_map/all_gather | solution.py:46
  326.0 13.2 %fusion.34 = f32[2,2048,128]{1,2,0:T(8,128)S(1)} fusion(bf16[1,2,4096,2048]{3,2,1,0:T(8,128)(2,1)} %param.5, bf16[4096,128]{0,1:T(8,128)(2,1)} %all-gather.9.cloned.1.call-done), kind=kOutput, calls=%fused_computation.22 | convolution fusion | flops 4294967296 | bytes 36700160 | tf_op jit(solution)/shard_map/kij,ib->kjb/dot_general | solution.py:43
  340.2 14.3 %reduce-scatter.19.cloned.1.call-done = bf16[1024,128]{0,1:T(8,128)(2,1)} async-done(((bf16[2048,128]{0,1:T(8,128)(2,1)}), bf16[1024,128]{0,1:T(8,128)(2,1)}) %reduce-scatter.19.cloned.1.call-update) | async-done | bytes 262160 | tf_op jit(solution)/shard_map/reduce_scatter | solution.py:50
  358.5 6.1 %all_gather.30 = bf16[2048,128]{0,1:T(8,128)(2,1)S(1)} all-gather(bf16[1024,128]{0,1:T(8,128)(2,1)S(1)} %fusion.71), channel_id=1, replica_groups=mesh['sec'=4,'row'=4,'col'=2] {'col'}, dimensions={0}, use_global_device_ids=true | all-gather | bytes 786432 | tf_op jit(solution)/shard_map/all_gather | solution.py:33
  364.6 16.3 %fusion.25 = f32[2,4096,128]{1,2,0:T(8,128)S(1)} fusion(bf16[1,2,4096,2048]{3,2,1,0:T(8,128)(2,1)} %param.5, bf16[2048,128]{0,1:T(8,128)(2,1)S(1)} %all_gather.30), kind=kOutput, calls=%fused_computation.19 | convolution fusion | flops 4294967296 | bytes 38273024 | tf_op jit(solution)/shard_map/kij,jb->kib/dot_general | solution.py:30
  382.3 32.3 %reduce-scatter.21.cloned.1.call-done = bf16[1024,128]{0,1:T(8,128)(2,1)} async-done(((bf16[4096,128]{0,1:T(8,128)(2,1)}), bf16[1024,128]{0,1:T(8,128)(2,1)}) %reduce-scatter.21.cloned.1.call-update) | async-done | bytes 262160 | tf_op jit(solution)/shard_map/reduce_scatter | solution.py:37
  416.4 26.7 %all-gather.11.cloned.1.call-done = bf16[4096,128]{0,1:T(8,128)(2,1)} async-done(((bf16[1024,128]{0,1:T(8,128)(2,1)}), bf16[4096,128]{0,1:T(8,128)(2,1)}) %all-gather.11.cloned.1.call-update) | async-done | bytes 1048592 | tf_op jit(solution)/shard_map/all_gather | solution.py:46
  443.2 13.2 %fusion.37 = f32[2,2048,128]{1,2,0:T(8,128)S(1)} fusion(bf16[1,2,4096,2048]{3,2,1,0:T(8,128)(2,1)} %param.5, bf16[4096,128]{0,1:T(8,128)(2,1)} %all-gather.11.cloned.1.call-done), kind=kOutput, calls=%fused_computation.23 | convolution fusion | flops 4294967296 | bytes 36700160 | tf_op jit(solution)/shard_map/kij,ib->kjb/dot_general | solution.py:43
  457.4 14.3 %reduce-scatter.23.cloned.1.call-done = bf16[1024,128]{0,1:T(8,128)(2,1)} async-done(((bf16[2048,128]{0,1:T(8,128)(2,1)}), bf16[1024,128]{0,1:T(8,128)(2,1)}) %reduce-scatter.23.cloned.1.call-update) | async-done | bytes 262160 | tf_op jit(solution)/shard_map/reduce_scatter | solution.py:50
  (82 shorter events, 33.8 us)
Async XLA Ops:
  6.5 56.9 %reduce-scatter.9.cloned.1.call-start = ((), (), s32[]{:S(2)}) async-start(), calls=%async_computation.8 | async-start | bytes 1310720 | tf_op jit(solution)/shard_map/reduce_scatter | solution.py:37
  34.2 57.9 %all-gather.5.cloned.1.call-start = ((), (), s32[]{:S(2)}) async-start(), calls=%async_computation.9 | async-start | bytes 1310720 | tf_op jit(solution)/shard_map/all_gather | solution.py:46
  65.3 55.3 %reduce-scatter.11.cloned.1.call-start = ((), (), s32[]{:S(2)}) async-start(), calls=%async_computation.10 | async-start | bytes 786432 | tf_op jit(solution)/shard_map/reduce_scatter | solution.py:50
  106.2 74.2 %reduce-scatter.13.cloned.1.call-start = ((), (), s32[]{:S(2)}) async-start(), calls=%async_computation.11 | async-start | bytes 1310720 | tf_op jit(solution)/shard_map/reduce_scatter | solution.py:37
  120.6 3.8 collective-permute-start
  148.1 61.0 %all-gather.7.cloned.1.call-start = ((), (), s32[]{:S(2)}) async-start(), calls=%async_computation.12 | async-start | bytes 1310720 | tf_op jit(solution)/shard_map/all_gather | solution.py:46
  182.2 55.3 %reduce-scatter.15.cloned.1.call-start = ((), (), s32[]{:S(2)}) async-start(), calls=%async_computation.13 | async-start | bytes 786432 | tf_op jit(solution)/shard_map/reduce_scatter | solution.py:50
  223.2 74.2 %reduce-scatter.17.cloned.1.call-start = ((), (), s32[]{:S(2)}) async-start(), calls=%async_computation.14 | async-start | bytes 1310720 | tf_op jit(solution)/shard_map/reduce_scatter | solution.py:37
  237.5 3.8 collective-permute-start.1
  265.0 60.9 %all-gather.9.cloned.1.call-start = ((), (), s32[]{:S(2)}) async-start(), calls=%async_computation.15 | async-start | bytes 1310720 | tf_op jit(solution)/shard_map/all_gather | solution.py:46
  299.2 55.3 %reduce-scatter.19.cloned.1.call-start = ((), (), s32[]{:S(2)}) async-start(), calls=%async_computation.16 | async-start | bytes 786432 | tf_op jit(solution)/shard_map/reduce_scatter | solution.py:50
  340.2 74.4 %reduce-scatter.21.cloned.1.call-start = ((), (), s32[]{:S(2)}) async-start(), calls=%async_computation.17 | async-start | bytes 1310720 | tf_op jit(solution)/shard_map/reduce_scatter | solution.py:37
  354.5 3.8 collective-permute-start.2
  382.2 60.9 %all-gather.11.cloned.1.call-start = ((), (), s32[]{:S(2)}) async-start(), calls=%async_computation.18 | async-start | bytes 1310720 | tf_op jit(solution)/shard_map/all_gather | solution.py:46
  416.4 55.3 %reduce-scatter.23.cloned.1.call-start = ((), (), s32[]{:S(2)}) async-start(), calls=%async_computation.19 | async-start | bytes 786432 | tf_op jit(solution)/shard_map/reduce_scatter | solution.py:50
  456.4 15.4 %copy-start = (bf16[1024,128]{0,1:T(8,128)(2,1)S(1)}, bf16[1024,128]{0,1:T(8,128)(2,1)}, u32[]{:S(2)}) copy-start(bf16[1024,128]{0,1:T(8,128)(2,1)} %reduce-scatter.11.cloned.1.call-done) | copy-start | bytes 786436
  456.4 15.4 %copy-start.1 = (bf16[1024,128]{0,1:T(8,128)(2,1)S(1)}, bf16[1024,128]{0,1:T(8,128)(2,1)}, u32[]{:S(2)}) copy-start(bf16[1024,128]{0,1:T(8,128)(2,1)} %reduce-scatter.15.cloned.1.call-done) | copy-start | bytes 786436
  456.4 15.3 %copy-start.2 = (bf16[1024,128]{0,1:T(8,128)(2,1)S(1)}, bf16[1024,128]{0,1:T(8,128)(2,1)}, u32[]{:S(2)}) copy-start(bf16[1024,128]{0,1:T(8,128)(2,1)} %reduce-scatter.19.cloned.1.call-done) | copy-start | bytes 786436
Sparse Core Ops, SparseCore 0:
  34.3 29.1 reduce-scatter.8
  65.4 26.6 all-gather.4
  106.3 14.1 reduce-scatter.10
  148.2 32.1 reduce-scatter.12
  182.4 26.6 all-gather.6
  223.3 14.1 reduce-scatter.14
  265.2 32.1 reduce-scatter.16
  299.4 26.5 all-gather.8
  340.3 14.1 reduce-scatter.18
  382.3 32.1 reduce-scatter.20
  416.5 26.5 all-gather.10
  457.5 14.1 reduce-scatter.22
where the time goes:
time: 483 us; the launch traced here: 481 us
  waiting for transfers between devices  297 us (61%)
  matrix products  118 us (24%)
  blocking collectives  25.8 us (5%)
  other arithmetic  17.6 us (4%)
  between operations  13.9 us (3%)
    reduce_scatter x4, waiting for transfers between devices, solve_section(): lax.psum_scatter(forward.astype(jnp.bfloat16), 'row', scatter_dimension=0...  125 us
    all_gather x4, waiting for transfers between devices, solve_section(): lax.all_gather(scaled, 'row', axis=0, tiled=True)  107 us
    dot_general x4, matrix products, solve_section(): jnp.einsum('kij,jb->kib', factor, lax.all_gather(source, 'col', axis=0, t...  65.2 us
    reduce_scatter x4, waiting for transfers between devices, solve_section(): lax.psum_scatter(back.astype(jnp.bfloat16), 'col', scatter_dimension=0, t...  57.2 us
    dot_general x4, matrix products, solve_section(): jnp.einsum('kij,ib->kjb', factor, lax.all_gather(scaled, 'row', axis=0, t...  52.8 us
    all_gather x4, blocking collectives, solve_section(): lax.all_gather(source, 'col', axis=0, tiled=True)  25.8 us
  transfers between devices with their start and end apart: 15, of which 15 were waited for; matrix products, arithmetic and copies ran while one was open for 0% of the time, Pallas kernels for 0%

commit v1 on v0

--- a/solution.py
+++ b/solution.py
@@ -1,6 +1,10 @@
+import functools
+
 import jax
 import jax.numpy as jnp
 from jax import lax
+from jax.experimental import pallas as pl
+from jax.experimental.pallas import tpu as pltpu
 from jax.sharding import PartitionSpec as P
 
 
@@ -88,6 +92,256 @@
     return results.reshape(1, rows_here, 2 * half)
 
 
+MESH = pl.DeviceIdType.MESH
+
+
+def sweep_kernel(
+    n_sec, n_row, n_col, forcing, dinv, coupling, factor_hbm, out,
+    factor, src_a, src_b, part_out, part_in, own, scaled, back,
+    cross_out, cross_in, prev_out, prev_in, forcing_t,
+    load_sem, src_send, src_recv, part_send, part_recv,
+    sc_send, sc_recv, cross_send, cross_recv, prev_send, prev_recv,
+):
+    share = own.shape[0]
+    half = own.shape[1] // 2
+    block_rows = n_row * share
+    block_cols = n_col * share
+    s, r, c = lax.axis_index("sec"), lax.axis_index("row"), lax.axis_index("col")
+
+    def meets(row, piece, col):
+        return row * block_cols < col * block_rows + (piece + 1) * share
+
+    def piece_rows(piece):
+        return pl.ds(pl.multiple_of(piece * share, share), share)
+
+    def load(k):
+        rows = piece_rows(lax.rem(r + k, n_row))
+        return pltpu.make_async_copy(
+            factor_hbm.at[0, :, rows, :], factor.at[:, rows, :], load_sem.at[k]
+        )
+
+    def send_source(j):
+        return pltpu.make_async_remote_copy(
+            src_ref=src_a.at[piece_rows(c)], dst_ref=src_a.at[piece_rows(c)],
+            send_sem=src_send.at[j - 1], recv_sem=src_recv.at[j - 1],
+            device_id=(s, r, lax.rem(c + j, n_col)), device_id_type=MESH,
+        )
+
+    def send_part(k):
+        return pltpu.make_async_remote_copy(
+            src_ref=part_out.at[k - 1], dst_ref=part_in.at[k - 1],
+            send_sem=part_send.at[k - 1], recv_sem=part_recv.at[k - 1],
+            device_id=(s, lax.rem(r + k, n_row), c), device_id_type=MESH,
+        )
+
+    def send_scaled(k):
+        return pltpu.make_async_remote_copy(
+            src_ref=scaled.at[r], dst_ref=scaled.at[r],
+            send_sem=sc_send.at[k - 1], recv_sem=sc_recv.at[k - 1],
+            device_id=(s, lax.rem(r + k, n_row), c), device_id_type=MESH,
+        )
+
+    def send_cross(j):
+        return pltpu.make_async_remote_copy(
+            src_ref=cross_out.at[j - 1], dst_ref=cross_in.at[j - 1],
+            send_sem=cross_send.at[j - 1], recv_sem=cross_recv.at[j - 1],
+            device_id=(s, r, lax.rem(c + j, n_col)), device_id_type=MESH,
+        )
+
+    def send_prev():
+        return pltpu.make_async_remote_copy(
+            src_ref=prev_out, dst_ref=prev_in, send_sem=prev_send, recv_sem=prev_recv,
+            device_id=(lax.rem(s + 1, n_sec), r, c), device_id_type=MESH,
+        )
+
+    order = list(range(1, n_row)) + [0]
+    for k in order:
+        @pl.when(meets(r, lax.rem(r + k, n_row), c))
+        def _(k=k):
+            load(k).start()
+
+    barrier = pltpu.get_barrier_semaphore()
+    for k in range(1, n_row):
+        pl.semaphore_signal(barrier, 1, device_id=(s, lax.rem(r + k, n_row), c), device_id_type=MESH)
+    for j in range(1, n_col):
+        pl.semaphore_signal(barrier, 1, device_id=(s, r, lax.rem(c + j, n_col)), device_id_type=MESH)
+    for step in (1, n_sec - 1):
+        pl.semaphore_signal(barrier, 1, device_id=(lax.rem(s + step, n_sec), r, c), device_id_type=MESH)
+    pl.semaphore_wait(barrier, n_row + n_col)
+
+    def turned(value):
+        return jnp.concatenate([-value[:, half:], value[:, :half]], axis=1)
+
+    @pl.when(s == 0)
+    def _():
+        src_a[piece_rows(c), :] = forcing[0].astype(jnp.bfloat16)
+
+    @pl.when(s > 0)
+    def _():
+        forcing_t[...] = forcing[0].T
+        send_prev().wait_recv()
+        previous = prev_in[...].astype(jnp.float32)
+        p_re, p_im = previous[:half], previous[half:]
+        c_re, c_im = coupling[0, 0:1, :], coupling[0, 1:2, :]
+        new_re = forcing_t[:half] - (c_re * p_re - c_im * p_im)
+        new_im = forcing_t[half:] - (c_re * p_im + c_im * p_re)
+        new = jnp.concatenate([new_re, new_im], axis=0).T
+        src_a[piece_rows(c), :] = new.astype(jnp.bfloat16)
+
+    for j in range(1, n_col):
+        send_source(j).start()
+    for j in range(n_col):
+        if j > 0:
+            send_source(j).wait_recv()
+        rows = piece_rows(lax.rem(c - j + n_col, n_col))
+        src_b[rows, :] = turned(src_a[rows, :].astype(jnp.float32)).astype(jnp.bfloat16)
+
+    tile = min(512, share)
+    for k in order:
+        piece = lax.rem(r + k, n_row)
+        wanted = meets(r, piece, c)
+
+        @pl.when(wanted)
+        def _(k=k, piece=piece):
+            load(k).wait()
+
+            @pl.loop(0, share // tile)
+            def _(t):
+                rows = pl.ds(pl.multiple_of(piece * share + t * tile, tile), tile)
+                here = pl.ds(pl.multiple_of(t * tile, tile), tile)
+                total = jnp.dot(factor[0, rows, :], src_a[...], preferred_element_type=jnp.float32)
+                total += jnp.dot(factor[1, rows, :], src_b[...], preferred_element_type=jnp.float32)
+                if k == 0:
+                    own[here, :] = total
+                else:
+                    part_out[k - 1, here, :] = total.astype(jnp.bfloat16)
+
+            if k > 0:
+                send_part(k).start()
+
+        if k == 0:
+            @pl.when(jnp.logical_not(wanted))
+            def _():
+                own[...] = jnp.zeros_like(own)
+
+    for k in range(1, n_row):
+        @pl.when(meets(lax.rem(r - k + n_row, n_row), r, c))
+        def _(k=k):
+            send_part(k).wait_recv()
+            own[...] += part_in[k - 1].astype(jnp.float32)
+
+    forward = own[...].T
+    d_re, d_im = dinv[0, 0:1, piece_rows(r)], dinv[0, 1:2, piece_rows(r)]
+    f_re, f_im = forward[:half], forward[half:]
+    scaled[r] = jnp.concatenate(
+        [d_re * f_re - d_im * f_im, d_re * f_im + d_im * f_re], axis=0
+    ).astype(jnp.bfloat16)
+    for k in range(1, n_row):
+        @pl.when(meets(lax.rem(r + k, n_row), r, c))
+        def _(k=k):
+            send_scaled(k).start()
+
+    back[...] = jnp.zeros_like(back)
+    width = min(512, block_cols)
+    for k in range(n_row):
+        piece = lax.rem(r - k + n_row, n_row)
+
+        @pl.when(meets(r, piece, c))
+        def _(k=k, piece=piece):
+            if k > 0:
+                send_scaled(k).wait_recv()
+            rows = piece_rows(piece)
+            lhs = scaled[piece]
+            lhs_b = jnp.concatenate([-lhs[half:], lhs[:half]], axis=0)
+
+            @pl.loop(0, block_cols // width)
+            def _(t):
+                cols = pl.ds(pl.multiple_of(t * width, width), width)
+                total = jnp.dot(lhs, factor[0, rows, cols], preferred_element_type=jnp.float32)
+                total += jnp.dot(lhs_b, factor[1, rows, cols], preferred_element_type=jnp.float32)
+                back[:, cols] += total
+
+    filled = meets(r, n_row - 1, c)
+    for j in range(1, n_col):
+        @pl.when(filled)
+        def _(j=j):
+            cross_out[j - 1] = back[:, piece_rows(lax.rem(c + j, n_col))].astype(jnp.bfloat16)
+            send_cross(j).start()
+
+    forcing_t[...] = back[:, piece_rows(c)]
+    for j in range(1, n_col):
+        @pl.when(meets(r, n_row - 1, lax.rem(c - j + n_col, n_col)))
+        def _(j=j):
+            send_cross(j).wait_recv()
+            forcing_t[...] += cross_in[j - 1].astype(jnp.float32)
+
+    @pl.when(s < n_sec - 1)
+    def _():
+        prev_out[...] = forcing_t[...].astype(jnp.bfloat16)
+        send_prev().start()
+
+    out[0] = forcing_t[...].T
+
+    for j in range(1, n_col):
+        send_source(j).wait_send()
+
+        @pl.when(filled)
+        def _(j=j):
+            send_cross(j).wait_send()
+
+    for k in range(1, n_row):
+        @pl.when(meets(r, lax.rem(r + k, n_row), c))
+        def _(k=k):
+            send_part(k).wait_send()
+
+        @pl.when(meets(lax.rem(r + k, n_row), r, c))
+        def _(k=k):
+            send_scaled(k).wait_send()
+
+    @pl.when(s < n_sec - 1)
+    def _():
+        send_prev().wait_send()
+
+
+def sweep(n_sec, n_row, n_col, forcing, inverse_factor, diag_inverse, coupling):
+    share, width = forcing.shape[1:]
+    block_rows, block_cols = inverse_factor.shape[2:]
+    vmem = pl.BlockSpec(memory_space=pltpu.VMEM)
+    bf16, f32 = jnp.bfloat16, jnp.float32
+    dma = pltpu.SemaphoreType.DMA
+    rows_out, cols_out = max(n_row - 1, 1), max(n_col - 1, 1)
+    return pl.pallas_call(
+        functools.partial(sweep_kernel, n_sec, n_row, n_col),
+        out_shape=jax.ShapeDtypeStruct(forcing.shape, f32),
+        in_specs=[vmem, vmem, vmem, pl.BlockSpec(memory_space=pl.ANY)],
+        out_specs=vmem,
+        scratch_shapes=[
+            pltpu.VMEM((2, block_rows, block_cols), bf16),
+            pltpu.VMEM((block_cols, width), bf16),
+            pltpu.VMEM((block_cols, width), bf16),
+            pltpu.VMEM((rows_out, share, width), bf16),
+            pltpu.VMEM((rows_out, share, width), bf16),
+            pltpu.VMEM((share, width), f32),
+            pltpu.VMEM((n_row, width, share), bf16),
+            pltpu.VMEM((width, block_cols), f32),
+            pltpu.VMEM((cols_out, width, share), bf16),
+            pltpu.VMEM((cols_out, width, share), bf16),
+            pltpu.VMEM((width, share), bf16),
+            pltpu.VMEM((width, share), bf16),
+            pltpu.VMEM((width, share), f32),
+            dma((n_row,)),
+            dma((cols_out,)), dma((cols_out,)),
+            dma((rows_out,)), dma((rows_out,)),
+            dma((rows_out,)), dma((rows_out,)),
+            dma((cols_out,)), dma((cols_out,)),
+            dma, dma,
+        ],
+        compiler_params=pltpu.CompilerParams(
+            collective_id=0, has_side_effects=True, vmem_limit_bytes=56 * 2**20
+        ),
+    )(forcing, diag_inverse, coupling, inverse_factor)
+
+
 def solution(mesh):
     placed = (
         P("sec", ("row", "col"), None),
@@ -95,6 +349,15 @@
         P("sec", None, "col"),
         P("sec", None, ("row", "col")),
     )
+    n_sec, n_row, n_col = (mesh.shape[axis] for axis in ("sec", "row", "col"))
+
+    def body(forcing, inverse_factor, diag_inverse, coupling):
+        share, width = forcing.shape[1:]
+        fits = inverse_factor.size * 2 <= 32 * 2**20
+        if share % 128 or width % 128 or not fits or n_sec < 3:
+            return local(forcing, inverse_factor, diag_inverse, coupling)
+        return sweep(n_sec, n_row, n_col, forcing, inverse_factor, diag_inverse, coupling)
+
     return jax.shard_map(
-        local, mesh=mesh, in_specs=placed, out_specs=P("sec", ("row", "col"), None), check_vma=False
+        body, mesh=mesh, in_specs=placed, out_specs=P("sec", ("row", "col"), None), check_vma=False
     )

time: 483 us -> 170 us (0.35)
  waiting for transfers between devices: 297 us -> 0 us
  Pallas kernels: 0 us -> 168 us
  matrix products: 118 us -> 0 us
  blocking collectives: 25.8 us -> 0 us
  other arithmetic: 17.6 us -> 0 us
  between operations: 13.9 us -> 0.01 us
    reduce_scatter x8 -> x0, waiting for transfers between devices: 183 us -> none  [the longest x4 125 us: solve_section(): lax.psum_scatter(forward.astype(jnp.bfloat16), 'row', scatter_dimension=0...]
    pallas_call x0 -> x1, Pallas kernels: none -> 168 us  [sweep(): pl.pallas_call(functools.partial(sweep_kernel, n_sec, n_row, n_col), out_...]
    dot_general x8 -> x0, matrix products: 118 us -> none  [the longest x4 65.2 us: solve_section(): jnp.einsum('kij,jb->kib', factor, lax.all_gather(source, 'col', axis=0, t...]
    all_gather x4 -> x0, waiting for transfers between devices: 107 us -> none  [solve_section(): lax.all_gather(scaled, 'row', axis=0, tiled=True)]
    all_gather x4 -> x0, blocking collectives: 25.8 us -> none  [solve_section(): lax.all_gather(source, 'col', axis=0, tiled=True)]
    concatenate x12 -> x0, other arithmetic: 10.4 us -> none  [the longest x8 7.53 us: combine_stack(): return jnp.concatenate([out_re, out_im], axis=1)]
    ppermute x3 -> x0, waiting for transfers between devices: 7.54 us -> none  [shifted(): lax.ppermute(value, axis, [(source, source + steps) for source in range(i...]
  transfers between devices with their start and end apart: 15 -> 0, of which waited for: 15 -> 0; matrix products, arithmetic and copies ran while one was open for 0% -> 0% of each run, Pallas kernels for 0% -> 0%
where the time goes in v1:
time: 170 us
  Pallas kernels  168 us (99%)
  local copies, waits for them, and re-layouts  1.87 us (1%)
    pallas_call x1, Pallas kernels, sweep(): pl.pallas_call(functools.partial(sweep_kernel, n_sec, n_row, n_col), out_...  168 us

profile of v1, /device:TPU:3, one launch (start us, length us, event | category | flops | bytes accessed | tf_op | source)
XLA Modules:
  0.0 170.1 jit_solution(2013617386457876523)
XLA Ops:
  0.0 168.2 %shard_map.46 = f32[1,1024,128]{2,1,0:T(8,128)} custom-call(f32[1,1024,128]{2,1,0:T(8,128)} %forcing.1, f32[1,2,4096]{2,1,0:T(2,128)} %dinv.1, f32[1,2,1024]{2,1,0:T(2,128)} %coupling.1, bf16[1,2,4096,2048]{3,2,1,0:T(8,128)(2,1)} %factor_hbm.1), custom_call_target="tpu_custom_call" | custom-call | tf_op jit(solution)/shard_map/pallas_call | solution.py:313
  168.2 1.9 %copy.6 = f32[1,1024,128]{2,1,0:T(8,128)} copy(f32[1,1024,128]{2,1,0:T(8,128)} %shard_map.46) | data formatting | bytes 1048576

commit v2 on v0

--- a/solution.py
+++ b/solution.py
@@ -1,6 +1,10 @@
+import functools
+
 import jax
 import jax.numpy as jnp
 from jax import lax
+from jax.experimental import pallas as pl
+from jax.experimental.pallas import tpu as pltpu
 from jax.sharding import PartitionSpec as P
 
 
@@ -88,6 +92,311 @@
     return results.reshape(1, rows_here, 2 * half)
 
 
+MESH = pl.DeviceIdType.MESH
+
+
+def sweep_kernel(
+    n_sec, n_row, n_col, forcing, dinv, coupling, factor_hbm, out,
+    factor, src_a, src_b, part_out, part_in, own, scaled, back,
+    cross_out, cross_in, prev_out, prev_in, forcing_t,
+    coupling_all, result,
+    load_sem, src_send, src_recv, part_send, part_recv,
+    sc_send, sc_recv, cross_send, cross_recv, prev_send, prev_recv,
+    rhs_send, rhs_recv, coef_send, coef_recv,
+):
+    share = own.shape[1]
+    half = own.shape[2] // 2
+    block_rows = n_row * share
+    block_cols = n_col * share
+    s, r, c = lax.axis_index("sec"), lax.axis_index("row"), lax.axis_index("col")
+
+    def last_row(piece, col):
+        return jnp.minimum(n_row - 1, (col * block_rows + (piece + 1) * share - 1) // block_cols)
+
+    def piece_rows(piece):
+        return pl.ds(pl.multiple_of(piece * share, share), share)
+
+    def load(q):
+        rows = piece_rows(q)
+        return pltpu.make_async_copy(
+            factor_hbm.at[0, :, rows, :], factor.at[:, rows, :], load_sem.at[q]
+        )
+
+    last = [last_row(q, c) for q in range(n_row)]
+    owner = [(m + 1) // 2 for m in last]
+
+    def send_source(j):
+        return pltpu.make_async_remote_copy(
+            src_ref=src_a.at[piece_rows(c)], dst_ref=src_a.at[piece_rows(c)],
+            send_sem=src_send.at[j - 1], recv_sem=src_recv.at[j - 1],
+            device_id=(s, r, lax.rem(c + j, n_col)), device_id_type=MESH,
+        )
+
+    def send_part(q, sender):
+        return pltpu.make_async_remote_copy(
+            src_ref=part_out.at[q], dst_ref=part_in.at[q, sender],
+            send_sem=part_send.at[q], recv_sem=part_recv.at[q, sender],
+            device_id=(s, owner[q], c), device_id_type=MESH,
+        )
+
+    def send_scaled(q, to):
+        return pltpu.make_async_remote_copy(
+            src_ref=scaled.at[q], dst_ref=scaled.at[q],
+            send_sem=sc_send.at[q, to], recv_sem=sc_recv.at[q],
+            device_id=(s, to, c), device_id_type=MESH,
+        )
+
+    def send_rhs(j):
+        return pltpu.make_async_remote_copy(
+            src_ref=forcing_t.at[c], dst_ref=forcing_t.at[c],
+            send_sem=rhs_send.at[j - 1], recv_sem=rhs_recv.at[j - 1],
+            device_id=(s, r, lax.rem(c + j, n_col)), device_id_type=MESH,
+        )
+
+    def send_coef(j):
+        return pltpu.make_async_remote_copy(
+            src_ref=coupling_all.at[c], dst_ref=coupling_all.at[c],
+            send_sem=coef_send.at[j - 1], recv_sem=coef_recv.at[j - 1],
+            device_id=(s, r, lax.rem(c + j, n_col)), device_id_type=MESH,
+        )
+
+    def send_cross(j):
+        return pltpu.make_async_remote_copy(
+            src_ref=cross_out.at[j - 1], dst_ref=cross_in.at[j - 1],
+            send_sem=cross_send.at[j - 1], recv_sem=cross_recv.at[j - 1],
+            device_id=(s, r, lax.rem(c + j, n_col)), device_id_type=MESH,
+        )
+
+    def send_prev(j):
+        return pltpu.make_async_remote_copy(
+            src_ref=prev_out, dst_ref=prev_in.at[j],
+            send_sem=prev_send.at[j], recv_sem=prev_recv.at[j],
+            device_id=(lax.rem(s + 1, n_sec), r, lax.rem(c + j, n_col)), device_id_type=MESH,
+        )
+
+    order = list(range(n_row - 1, -1, -1))
+    for q in order:
+        @pl.when(r <= last[q])
+        def _(q=q):
+            load(q).start()
+
+    barrier = pltpu.get_barrier_semaphore()
+    for i in range(1, n_row):
+        pl.semaphore_signal(barrier, 1, device_id=(s, lax.rem(r + i, n_row), c), device_id_type=MESH)
+    for j in range(1, n_col):
+        pl.semaphore_signal(barrier, 1, device_id=(s, r, lax.rem(c + j, n_col)), device_id_type=MESH)
+    for step in (1, n_sec - 1):
+        for j in range(n_col):
+            pl.semaphore_signal(
+                barrier, 1, device_id=(lax.rem(s + step, n_sec), r, lax.rem(c + j, n_col)),
+                device_id_type=MESH,
+            )
+    pl.semaphore_wait(barrier, n_row - 1 + n_col - 1 + 2 * n_col)
+
+    def turned(value):
+        return jnp.concatenate([-value[:, half:], value[:, :half]], axis=1)
+
+    @pl.when(s == 0)
+    def _():
+        src_a[piece_rows(c), :] = forcing[0].astype(jnp.bfloat16)
+        for j in range(1, n_col):
+            send_source(j).start()
+        for j in range(n_col):
+            if j > 0:
+                send_source(j).wait_recv()
+            rows = piece_rows(lax.rem(c - j + n_col, n_col))
+            src_b[rows, :] = turned(src_a[rows, :].astype(jnp.float32)).astype(jnp.bfloat16)
+
+    @pl.when(s > 0)
+    def _():
+        forcing_t[c] = forcing[0].T
+        coupling_all[c] = coupling[0]
+        for j in range(1, n_col):
+            send_rhs(j).start()
+            send_coef(j).start()
+        for j in range(1, n_col):
+            send_rhs(j).wait_recv()
+            send_coef(j).wait_recv()
+        for j in range(n_col):
+            col = lax.rem(c - j + n_col, n_col)
+            rows = piece_rows(col)
+            send_prev(j).wait_recv()
+            previous = prev_in[j].astype(jnp.float32)
+            p_re, p_im = previous[:half], previous[half:]
+            c_re, c_im = coupling_all[col, 0:1, :], coupling_all[col, 1:2, :]
+            new_re = forcing_t[col, :half] - (c_re * p_re - c_im * p_im)
+            new_im = forcing_t[col, half:] - (c_re * p_im + c_im * p_re)
+            src_a[rows, :] = jnp.concatenate([new_re, new_im], axis=0).T.astype(jnp.bfloat16)
+            src_b[rows, :] = jnp.concatenate([-new_im, new_re], axis=0).T.astype(jnp.bfloat16)
+
+    tile = min(512, share)
+
+    def forward_piece(q):
+        @pl.when(r <= last[q])
+        def _():
+            load(q).wait()
+            mine = r == owner[q]
+
+            @pl.loop(0, share // tile)
+            def _(t):
+                rows = pl.ds(pl.multiple_of(q * share + t * tile, tile), tile)
+                here = pl.ds(pl.multiple_of(t * tile, tile), tile)
+                total = jnp.dot(factor[0, rows, :], src_a[...], preferred_element_type=jnp.float32)
+                total += jnp.dot(factor[1, rows, :], src_b[...], preferred_element_type=jnp.float32)
+                own[q, here, :] = total
+                part_out[q, here, :] = total.astype(jnp.bfloat16)
+
+            @pl.when(jnp.logical_not(mine))
+            def _():
+                send_part(q, r).start()
+
+    def reduce_piece(q):
+        @pl.when(r == owner[q])
+        def _():
+            for p in range(n_row):
+                @pl.when(jnp.logical_and(p != r, p <= last[q]))
+                def _(p=p):
+                    send_part(q, p).wait_recv()
+                    own[q] += part_in[q, p].astype(jnp.float32)
+
+            forward = own[q].T
+            d_re, d_im = dinv[0, 0:1, pl.ds(q * share, share)], dinv[0, 1:2, pl.ds(q * share, share)]
+            f_re, f_im = forward[:half], forward[half:]
+            scaled[q] = jnp.concatenate(
+                [d_re * f_re - d_im * f_im, d_re * f_im + d_im * f_re], axis=0
+            ).astype(jnp.bfloat16)
+            for p in range(n_row):
+                @pl.when(jnp.logical_and(p != r, p <= last[q]))
+                def _(p=p):
+                    send_scaled(q, p).start()
+
+    for i, q in enumerate(order):
+        forward_piece(q)
+        if i >= 2:
+            reduce_piece(order[i - 2])
+    for q in order[max(n_row - 2, 0):]:
+        reduce_piece(q)
+
+    back[...] = jnp.zeros_like(back)
+    width = min(512, share)
+    filled = r <= last[n_row - 1]
+    turns = list(range(1, n_row, 2)) + list(range(0, n_row, 2))
+    for q in turns:
+        @pl.when(jnp.logical_and(r <= last[q], r != owner[q]))
+        def _(q=q):
+            send_scaled(q, r).wait_recv()
+
+        for j in list(range(1, n_col)) + [0]:
+            @pl.when(r <= last[q])
+            def _(q=q, j=j):
+                rows = piece_rows(q)
+                lhs = scaled[q]
+                lhs_b = jnp.concatenate([-lhs[half:], lhs[:half]], axis=0)
+
+                @pl.loop(0, share // width)
+                def _(t):
+                    first = lax.rem(c + j, n_col) * share + t * width
+                    cols = pl.ds(pl.multiple_of(first, width), width)
+                    total = jnp.dot(lhs, factor[0, rows, cols], preferred_element_type=jnp.float32)
+                    total += jnp.dot(lhs_b, factor[1, rows, cols], preferred_element_type=jnp.float32)
+                    back[:, cols] += total
+
+            if q == turns[-1] and j > 0:
+                @pl.when(filled)
+                def _(j=j):
+                    cross_out[j - 1] = back[:, piece_rows(lax.rem(c + j, n_col))].astype(jnp.bfloat16)
+                    send_cross(j).start()
+
+    result[...] = back[:, piece_rows(c)]
+    for j in range(1, n_col):
+        @pl.when(r <= last_row(n_row - 1, lax.rem(c - j + n_col, n_col)))
+        def _(j=j):
+            send_cross(j).wait_recv()
+            result[...] += cross_in[j - 1].astype(jnp.float32)
+
+    @pl.when(s < n_sec - 1)
+    def _():
+        prev_out[...] = result[...].astype(jnp.bfloat16)
+        for j in list(range(1, n_col)) + [0]:
+            send_prev(j).start()
+
+    out[0] = result[...].T
+
+    @pl.when(s == 0)
+    def _():
+        for j in range(1, n_col):
+            send_source(j).wait_send()
+
+    @pl.when(s > 0)
+    def _():
+        for j in range(1, n_col):
+            send_rhs(j).wait_send()
+            send_coef(j).wait_send()
+
+    @pl.when(filled)
+    def _():
+        for j in range(1, n_col):
+            send_cross(j).wait_send()
+
+    for q in range(n_row):
+        @pl.when(jnp.logical_and(r <= last[q], r != owner[q]))
+        def _(q=q):
+            send_part(q, r).wait_send()
+
+        for p in range(n_row):
+            @pl.when(jnp.logical_and(r == owner[q], jnp.logical_and(p != r, p <= last[q])))
+            def _(q=q, p=p):
+                send_scaled(q, p).wait_send()
+
+    @pl.when(s < n_sec - 1)
+    def _():
+        for j in range(n_col):
+            send_prev(j).wait_send()
+
+
+def sweep(n_sec, n_row, n_col, forcing, inverse_factor, diag_inverse, coupling):
+    share, width = forcing.shape[1:]
+    block_rows, block_cols = inverse_factor.shape[2:]
+    vmem = pl.BlockSpec(memory_space=pltpu.VMEM)
+    bf16, f32 = jnp.bfloat16, jnp.float32
+    dma = pltpu.SemaphoreType.DMA
+    cols_out = max(n_col - 1, 1)
+    return pl.pallas_call(
+        functools.partial(sweep_kernel, n_sec, n_row, n_col),
+        out_shape=jax.ShapeDtypeStruct(forcing.shape, f32),
+        in_specs=[vmem, vmem, vmem, pl.BlockSpec(memory_space=pl.ANY)],
+        out_specs=vmem,
+        scratch_shapes=[
+            pltpu.VMEM((2, block_rows, block_cols), bf16),
+            pltpu.VMEM((block_cols, width), bf16),
+            pltpu.VMEM((block_cols, width), bf16),
+            pltpu.VMEM((n_row, share, width), bf16),
+            pltpu.VMEM((n_row, n_row, share, width), bf16),
+            pltpu.VMEM((n_row, share, width), f32),
+            pltpu.VMEM((n_row, width, share), bf16),
+            pltpu.VMEM((width, block_cols), f32),
+            pltpu.VMEM((cols_out, width, share), bf16),
+            pltpu.VMEM((cols_out, width, share), bf16),
+            pltpu.VMEM((width, share), bf16),
+            pltpu.VMEM((n_col, width, share), bf16),
+            pltpu.VMEM((n_col, width, share), f32),
+            pltpu.VMEM((n_col, 2, share), f32),
+            pltpu.VMEM((width, share), f32),
+            dma((n_row,)),
+            dma((cols_out,)), dma((cols_out,)),
+            dma((n_row,)), dma((n_row, n_row)),
+            dma((n_row, n_row)), dma((n_row,)),
+            dma((cols_out,)), dma((cols_out,)),
+            dma((n_col,)), dma((n_col,)),
+            dma((cols_out,)), dma((cols_out,)),
+            dma((cols_out,)), dma((cols_out,)),
+        ],
+        compiler_params=pltpu.CompilerParams(
+            collective_id=0, has_side_effects=True, vmem_limit_bytes=56 * 2**20
+        ),
+    )(forcing, diag_inverse, coupling, inverse_factor)
+
+
 def solution(mesh):
     placed = (
         P("sec", ("row", "col"), None),
@@ -95,6 +404,15 @@
         P("sec", None, "col"),
         P("sec", None, ("row", "col")),
     )
+    n_sec, n_row, n_col = (mesh.shape[axis] for axis in ("sec", "row", "col"))
+
+    def body(forcing, inverse_factor, diag_inverse, coupling):
+        share, width = forcing.shape[1:]
+        fits = inverse_factor.size * 2 <= 32 * 2**20
+        if share % 128 or width % 128 or not fits or n_sec < 3:
+            return local(forcing, inverse_factor, diag_inverse, coupling)
+        return sweep(n_sec, n_row, n_col, forcing, inverse_factor, diag_inverse, coupling)
+
     return jax.shard_map(
-        local, mesh=mesh, in_specs=placed, out_specs=P("sec", ("row", "col"), None), check_vma=False
+        body, mesh=mesh, in_specs=placed, out_specs=P("sec", ("row", "col"), None), check_vma=False
     )

time: 483 us -> 177 us (0.37)
  waiting for transfers between devices: 297 us -> 0 us
  Pallas kernels: 0 us -> 175 us
  matrix products: 118 us -> 0 us
  blocking collectives: 25.8 us -> 0 us
  other arithmetic: 17.6 us -> 0 us
  between operations: 13.9 us -> 0.01 us
    reduce_scatter x8 -> x0, waiting for transfers between devices: 183 us -> none  [the longest x4 125 us: solve_section(): lax.psum_scatter(forward.astype(jnp.bfloat16), 'row', scatter_dimension=0...]
    pallas_call x0 -> x1, Pallas kernels: none -> 175 us  [sweep(): pl.pallas_call(functools.partial(sweep_kernel, n_sec, n_row, n_col), out_...]
    dot_general x8 -> x0, matrix products: 118 us -> none  [the longest x4 65.2 us: solve_section(): jnp.einsum('kij,jb->kib', factor, lax.all_gather(source, 'col', axis=0, t...]
    all_gather x4 -> x0, waiting for transfers between devices: 107 us -> none  [solve_section(): lax.all_gather(scaled, 'row', axis=0, tiled=True)]
    all_gather x4 -> x0, blocking collectives: 25.8 us -> none  [solve_section(): lax.all_gather(source, 'col', axis=0, tiled=True)]
    concatenate x12 -> x0, other arithmetic: 10.4 us -> none  [the longest x8 7.53 us: combine_stack(): return jnp.concatenate([out_re, out_im], axis=1)]
    ppermute x3 -> x0, waiting for transfers between devices: 7.54 us -> none  [shifted(): lax.ppermute(value, axis, [(source, source + steps) for source in range(i...]
  transfers between devices with their start and end apart: 15 -> 0, of which waited for: 15 -> 0; matrix products, arithmetic and copies ran while one was open for 0% -> 0% of each run, Pallas kernels for 0% -> 0%
where the time goes in v2:
time: 177 us
  Pallas kernels  175 us (99%)
  local copies, waits for them, and re-layouts  1.87 us (1%)
    pallas_call x1, Pallas kernels, sweep(): pl.pallas_call(functools.partial(sweep_kernel, n_sec, n_row, n_col), out_...  175 us

profile of v2, /device:TPU:3, one launch (start us, length us, event | category | flops | bytes accessed | tf_op | source)
XLA Modules:
  0.0 176.8 jit_solution(2020630479299891929)
XLA Ops:
  0.0 174.9 %shard_map.46 = f32[1,1024,128]{2,1,0:T(8,128)} custom-call(f32[1,1024,128]{2,1,0:T(8,128)} %forcing.1, f32[1,2,4096]{2,1,0:T(2,128)} %dinv.1, f32[1,2,1024]{2,1,0:T(2,128)} %coupling.1, bf16[1,2,4096,2048]{3,2,1,0:T(8,128)(2,1)} %factor_hbm.1), custom_call_target="tpu_custom_call" | custom-call | tf_op jit(solution)/shard_map/pallas_call | solution.py:364
  175.0 1.9 %copy.6 = f32[1,1024,128]{2,1,0:T(8,128)} copy(f32[1,1024,128]{2,1,0:T(8,128)} %shard_map.46) | data formatting | bytes 1048576

commit v3 on v2

--- a/solution.py
+++ b/solution.py
@@ -132,19 +132,35 @@
             device_id=(s, r, lax.rem(c + j, n_col)), device_id_type=MESH,
         )
 
-    def send_part(q, sender):
-        return pltpu.make_async_remote_copy(
-            src_ref=part_out.at[q], dst_ref=part_in.at[q, sender],
-            send_sem=part_send.at[q], recv_sem=part_recv.at[q, sender],
-            device_id=(s, owner[q], c), device_id_type=MESH,
-        )
-
-    def send_scaled(q, to):
+    inner = [
+        jnp.logical_and(r != o, jnp.logical_and(r > 0, jnp.logical_or(r < o, r < m)))
+        for o, m in zip(owner, last)
+    ]
+
+    def send_part(q, side):
+        return pltpu.make_async_remote_copy(
+            src_ref=part_out.at[q], dst_ref=part_in.at[q, side],
+            send_sem=part_send.at[q], recv_sem=part_recv.at[q, side],
+            device_id=(s, lax.rem(r + (1 if side == 0 else n_row - 1), n_row), c), device_id_type=MESH,
+        )
+
+    def start_part(q):
+        for side in (0, 1):
+            @pl.when((r < owner[q]) if side == 0 else (r > owner[q]))
+            def _(side=side):
+                send_part(q, side).start()
+
+    def send_scaled(q, side):
         return pltpu.make_async_remote_copy(
             src_ref=scaled.at[q], dst_ref=scaled.at[q],
-            send_sem=sc_send.at[q, to], recv_sem=sc_recv.at[q],
-            device_id=(s, to, c), device_id_type=MESH,
-        )
+            send_sem=sc_send.at[q, side], recv_sem=sc_recv.at[q],
+            device_id=(s, lax.rem(r + (1 if side == 0 else n_row - 1), n_row), c), device_id_type=MESH,
+        )
+
+    def passes_on(q, side):
+        if side == 0:
+            return jnp.logical_and(r >= owner[q], r < last[q])
+        return jnp.logical_and(r <= owner[q], r > 0)
 
     def send_rhs(j):
         return pltpu.make_async_remote_copy(
@@ -235,8 +251,6 @@
         @pl.when(r <= last[q])
         def _():
             load(q).wait()
-            mine = r == owner[q]
-
             @pl.loop(0, share // tile)
             def _(t):
                 rows = pl.ds(pl.multiple_of(q * share + t * tile, tile), tile)
@@ -246,18 +260,37 @@
                 own[q, here, :] = total
                 part_out[q, here, :] = total.astype(jnp.bfloat16)
 
-            @pl.when(jnp.logical_not(mine))
+            @pl.when(jnp.logical_and(r != owner[q], jnp.logical_not(inner[q])))
             def _():
-                send_part(q, r).start()
+                start_part(q)
+
+    def relay_part(q):
+        for side in (0, 1):
+            between = jnp.logical_and(r > 0, r < owner[q])
+            if side == 1:
+                between = jnp.logical_and(r > owner[q], r < last[q])
+
+            @pl.when(between)
+            def _(side=side):
+                send_part(q, side).wait_recv()
+                part_out[q] = (own[q] + part_in[q, side].astype(jnp.float32)).astype(jnp.bfloat16)
+                send_part(q, side).start()
+
+    def relay_scaled(q):
+        for side in (0, 1):
+            @pl.when(jnp.logical_and(passes_on(q, side), r != owner[q]))
+            def _(side=side):
+                send_scaled(q, side).wait_recv()
+                send_scaled(q, side).start()
 
     def reduce_piece(q):
         @pl.when(r == owner[q])
         def _():
-            for p in range(n_row):
-                @pl.when(jnp.logical_and(p != r, p <= last[q]))
-                def _(p=p):
-                    send_part(q, p).wait_recv()
-                    own[q] += part_in[q, p].astype(jnp.float32)
+            for side in (0, 1):
+                @pl.when((r > 0) if side == 0 else (r < last[q]))
+                def _(side=side):
+                    send_part(q, side).wait_recv()
+                    own[q] += part_in[q, side].astype(jnp.float32)
 
             forward = own[q].T
             d_re, d_im = dinv[0, 0:1, pl.ds(q * share, share)], dinv[0, 1:2, pl.ds(q * share, share)]
@@ -265,26 +298,34 @@
             scaled[q] = jnp.concatenate(
                 [d_re * f_re - d_im * f_im, d_re * f_im + d_im * f_re], axis=0
             ).astype(jnp.bfloat16)
-            for p in range(n_row):
-                @pl.when(jnp.logical_and(p != r, p <= last[q]))
-                def _(p=p):
-                    send_scaled(q, p).start()
+            for side in (0, 1):
+                @pl.when(passes_on(q, side))
+                def _(side=side):
+                    send_scaled(q, side).start()
 
     for i, q in enumerate(order):
         forward_piece(q)
-        if i >= 2:
-            reduce_piece(order[i - 2])
-    for q in order[max(n_row - 2, 0):]:
+        if i >= 1:
+            relay_part(order[i - 1])
+    relay_part(order[-1])
+    for q in order:
         reduce_piece(q)
 
     back[...] = jnp.zeros_like(back)
     width = min(512, share)
     filled = r <= last[n_row - 1]
     turns = list(range(1, n_row, 2)) + list(range(0, n_row, 2))
-    for q in turns:
-        @pl.when(jnp.logical_and(r <= last[q], r != owner[q]))
+    relayed = []
+    for i, q in enumerate(turns):
+        for piece in (order[i], q):
+            if piece not in relayed:
+                relayed.append(piece)
+                relay_scaled(piece)
+        ends = jnp.logical_or(r == last[q], r == 0)
+
+        @pl.when(jnp.logical_and(jnp.logical_and(r <= last[q], r != owner[q]), ends))
         def _(q=q):
-            send_scaled(q, r).wait_recv()
+            send_scaled(q, 0).wait_recv()
 
         for j in list(range(1, n_col)) + [0]:
             @pl.when(r <= last[q])
@@ -341,12 +382,12 @@
     for q in range(n_row):
         @pl.when(jnp.logical_and(r <= last[q], r != owner[q]))
         def _(q=q):
-            send_part(q, r).wait_send()
-
-        for p in range(n_row):
-            @pl.when(jnp.logical_and(r == owner[q], jnp.logical_and(p != r, p <= last[q])))
-            def _(q=q, p=p):
-                send_scaled(q, p).wait_send()
+            send_part(q, 0).wait_send()
+
+        for side in (0, 1):
+            @pl.when(passes_on(q, side))
+            def _(q=q, side=side):
+                send_scaled(q, side).wait_send()
 
     @pl.when(s < n_sec - 1)
     def _():
@@ -371,7 +412,7 @@
             pltpu.VMEM((block_cols, width), bf16),
             pltpu.VMEM((block_cols, width), bf16),
             pltpu.VMEM((n_row, share, width), bf16),
-            pltpu.VMEM((n_row, n_row, share, width), bf16),
+            pltpu.VMEM((n_row, 2, share, width), bf16),
             pltpu.VMEM((n_row, share, width), f32),
             pltpu.VMEM((n_row, width, share), bf16),
             pltpu.VMEM((width, block_cols), f32),
@@ -384,8 +425,8 @@
             pltpu.VMEM((width, share), f32),
             dma((n_row,)),
             dma((cols_out,)), dma((cols_out,)),
-            dma((n_row,)), dma((n_row, n_row)),
-            dma((n_row, n_row)), dma((n_row,)),
+            dma((n_row,)), dma((n_row, 2)),
+            dma((n_row, 2)), dma((n_row,)),
             dma((cols_out,)), dma((cols_out,)),
             dma((n_col,)), dma((n_col,)),
             dma((cols_out,)), dma((cols_out,)),

time: 177 us -> 167 us (0.944)
  Pallas kernels: 175 us -> 165 us
    pallas_call x1, Pallas kernels: 175 us -> 165 us  [sweep(): pl.pallas_call(functools.partial(sweep_kernel, n_sec, n_row, n_col), out_...]
where the time goes in v3:
time: 167 us; the launch traced here: 166 us
  Pallas kernels  165 us (99%)
  local copies, waits for them, and re-layouts  1.87 us (1%)
    pallas_call x1, Pallas kernels, sweep(): pl.pallas_call(functools.partial(sweep_kernel, n_sec, n_row, n_col), out_...  165 us

profile of v3, /device:TPU:3, one launch (start us, length us, event | category | flops | bytes accessed | tf_op | source)
XLA Modules:
  0.0 166.5 jit_solution(11656499163601020107)
XLA Ops:
  0.0 164.6 %shard_map.46 = f32[1,1024,128]{2,1,0:T(8,128)} custom-call(f32[1,1024,128]{2,1,0:T(8,128)} %forcing.1, f32[1,2,4096]{2,1,0:T(2,128)} %dinv.1, f32[1,2,1024]{2,1,0:T(2,128)} %coupling.1, bf16[1,2,4096,2048]{3,2,1,0:T(8,128)(2,1)} %factor_hbm.1), custom_call_target="tpu_custom_call" | custom-call | tf_op jit(solution)/shard_map/pallas_call | solution.py:405
  164.6 1.9 %copy.6 = f32[1,1024,128]{2,1,0:T(8,128)} copy(f32[1,1024,128]{2,1,0:T(8,128)} %shard_map.46) | data formatting | bytes 1048576
